TPU v7x, 32 devices: a whole 2x2x4 slice. The times are simulated.
32 devices in a mesh: visit: 2 (over x), patch: 16 (over z, y, core).
Axes of the slice: x: 2, y: 2, z: 4, core: 2. Of those that a mesh axis runs over, the one named last changes fastest.
Arguments:
- images: bfloat16 [2, 96, 128, 512], P('visit', 'patch'), may hold values from -12 to 12
- coefficients: float32 [2, 96, 3, 40], P('visit', 'patch'), may hold values from -2 to 2
- intersection: int32 [2, 96, 2], P('visit'), may hold values from 0 to 15, as said below
- row_offset: int32 [2, 96], P('visit'), may hold values from 0 to 7
- col_offset: int32 [2, 96], P('visit'), may hold values from 0 to 511
- shifts: float32 [2, 96, 2], P('visit'), may hold values from 0 to 1
- inv_var: float32 [2, 96], P('visit'), may hold values from 0.3 to 3
Outputs:
- coadd: float32 [128, 8192], P('visit', 'patch')
- detection: float32 [128, 8192], P('visit', 'patch')
Inputs may be any that keep to these rules, and one draw needn't show every extreme that they name: intersection[v, c, 1] = intersection[v, c, 0] + 1. Within each aligned block of 6 exposures of a visit (c from b * 6 to (b + 1) * 6 - 1), no patch is named twice.
All inputs are finite; a program needn't handle non-finite values.
Results may differ from a plain program's by a relative error of at most 0.0061.
Values may be sent and summed in bfloat16 or wider, within the bound.
No kernel may reach another device: no remote copies, remote signals or barrier semaphores. Data moves between devices by JAX's collectives and lax.ppermute only.
A program may use at most 128 MiB of HBM per device.

v0:
```python
import jax
import jax.numpy as jnp
from jax import lax
from jax.sharding import PartitionSpec as P

KRAD = 10
DRAD = 4
WIDTHS_PX = (1.0, 1.7, 2.6, 3.6)


def extended(array, sides, width):
    for axis, dim in sides:
        peers, length = (lax.axis_size(axis), array.shape[dim])
        up = [(i, (i + 1) % peers) for i in range(peers - 1)]
        down = [(j, i) for i, j in up]
        last = lax.slice_in_dim(array, length - width, length, axis=dim)
        initial = lax.slice_in_dim(array, 0, width, axis=dim)
        before = lax.ppermute(last, axis, up)
        after = lax.ppermute(initial, axis, down)
        array = jnp.concatenate([before, array, after], axis=dim)
    return array


def kernel_value(offsets, width_px, degree):
    scaled = offsets / width_px
    return scaled**degree * jnp.exp(-offsets * offsets / (2.0 * width_px * width_px))


def band_tables(radius, extent):
    offsets = jnp.arange(-radius, radius + 1).astype(jnp.float32)
    distance = (jnp.arange(extent)[None, :] - jnp.arange(extent)[:, None]).astype(jnp.float32)
    inside = jnp.abs(distance) <= radius
    tables = []
    for group in range(4):
        for degree in range(4):
            profile = kernel_value(offsets, WIDTHS_PX[group], degree)
            norm_value = jnp.sqrt(jnp.sum(profile * profile))
            values = kernel_value(distance, WIDTHS_PX[group], degree) / norm_value
            tables.append(jnp.where(inside, values, 0.0).astype(jnp.bfloat16))
    return jnp.stack(tables).reshape(4, 4, extent, extent)


def match_exposure(exposure, weights, row_band, col_band, row_pos, col_pos):
    smoothed = jnp.einsum(
        "gdri,iw->gdrw", row_band, exposure, preferred_element_type=jnp.float32
    ).astype(jnp.bfloat16)
    matched = jnp.zeros(exposure.shape, jnp.float32)
    term = 0
    for group in range(4):
        for x_degree in range(4):
            count = 4 - x_degree
            response = jnp.einsum(
                "drw,xw->drx",
                smoothed[group, :count],
                col_band[group, x_degree],
                preferred_element_type=jnp.float32,
            )
            picked = weights[:, term : term + count]
            steady = jnp.sum(picked[0][:, None, None] * response, 0)
            along_rows = jnp.sum(picked[1][:, None, None] * response, 0)
            along_cols = jnp.sum(picked[2][:, None, None] * response, 0)
            matched = (
                matched + steady + row_pos[:, None] * along_rows + col_pos[None, :] * along_cols
            )
            term += count
    return matched.astype(jnp.bfloat16)


def warp_exposure(exposure, row_shift, col_shift, frac_row, frac_col, weight):
    row_count, col_count = exposure.shape
    nothing = jnp.zeros((), jnp.bfloat16)
    upper = (1.0 - frac_row).astype(jnp.bfloat16)
    lower = frac_row.astype(jnp.bfloat16)
    left = (1.0 - frac_col).astype(jnp.bfloat16)
    right = frac_col.astype(jnp.bfloat16)
    target_row = jnp.arange(row_count)[:, None]
    source_row = jnp.arange(row_count)[None, :]
    row_map = jnp.where(source_row == target_row - row_shift, upper, nothing) + jnp.where(
        source_row == target_row - row_shift - 1, lower, nothing
    )
    source_col = jnp.arange(col_count)[:, None]
    target_col = jnp.arange(col_count)[None, :]
    col_map = jnp.where(source_col == target_col - col_shift, left, nothing) + jnp.where(
        source_col == target_col - col_shift - 1, right, nothing
    )
    middle = jnp.dot(row_map, exposure, preferred_element_type=jnp.float32).astype(jnp.bfloat16)
    warped = jnp.dot(middle, col_map, preferred_element_type=jnp.float32)
    row_cover = jnp.sum(row_map.astype(jnp.float32), 1)
    col_cover = jnp.sum(col_map.astype(jnp.float32), 0)
    return (weight * warped, weight * row_cover[:, None] * col_cover[None, :])


def detect(framed, radius):
    offsets = jnp.arange(-radius, radius + 1).astype(jnp.float32)
    profile = jnp.exp(-offsets * offsets / 8.0)
    profile = profile / jnp.sqrt(jnp.sum(profile * profile))
    row_count = framed.shape[0] - 2 * radius
    col_count = framed.shape[1] - 2 * radius
    across = jnp.zeros((row_count, framed.shape[1]), jnp.float32)
    for tap_idx in range(2 * radius + 1):
        across = across + profile[tap_idx] * framed[tap_idx : tap_idx + row_count]
    result = jnp.zeros((row_count, col_count), jnp.float32)
    for tap_idx in range(2 * radius + 1):
        result = result + profile[tap_idx] * across[:, tap_idx : tap_idx + col_count]
    return result


def local(images, coefficients, intersection, row_offset, col_offset, shifts, inv_var):
    exposures = images[0]
    weights_all = coefficients[0]
    row_count = exposures.shape[1]
    col_count = exposures.shape[2]
    table = intersection[0]
    row_shifts = row_offset[0]
    col_shifts = col_offset[0]
    fractions = shifts[0]
    inverse = inv_var[0]
    own_patch = lax.axis_index("patch")
    row_band = band_tables(KRAD, row_count)
    col_band = band_tables(KRAD, col_count)
    row_pos = (2.0 * jnp.arange(row_count).astype(jnp.float32) + 1.0) / row_count - 1.0
    col_pos = (2.0 * jnp.arange(col_count).astype(jnp.float32) + 1.0) / col_count - 1.0
    matched = lax.map(
        lambda operands: match_exposure(
            operands[0], operands[1], row_band, col_band, row_pos, col_pos
        ),
        (exposures, weights_all),
    )
    empty = (
        jnp.zeros((row_count, col_count), jnp.float32),
        jnp.zeros((row_count, col_count), jnp.float32),
    )

    def add_exposure(totals, exposure, ccd, hit_first):
        col_shift = jnp.where(hit_first, col_shifts[ccd], col_shifts[ccd] - col_count)
        flux_part, cover_part = warp_exposure(
            exposure, row_shifts[ccd], col_shift, fractions[ccd, 0], fractions[ccd, 1], inverse[ccd]
        )
        return (totals[0] + flux_part, totals[1] + cover_part)

    arrived = lax.all_gather(matched, "patch", axis=0, tiled=True)

    def visit_one(offset, inner):
        hit_first = table[offset, 0] == own_patch
        hit_second = table[offset, 1] == own_patch
        exposure = lax.dynamic_index_in_dim(arrived, offset, 0, keepdims=False)
        return lax.cond(
            hit_first | hit_second,
            lambda: add_exposure(inner, exposure, offset, hit_first),
            lambda: inner,
        )

    flux_sum, cover_sum = lax.fori_loop(0, arrived.shape[0], visit_one, empty)
    flux_part, cover_part = (
        lax.psum_scatter(flux_sum, "visit", scatter_dimension=0, tiled=True),
        lax.psum_scatter(cover_sum, "visit", scatter_dimension=0, tiled=True),
    )
    coadd = flux_part / jnp.maximum(cover_part, 1.0)
    framed = extended(coadd, (("visit", 0), ("patch", 1)), DRAD)
    detection = detect(framed, DRAD)
    return (coadd, detection)


def solution(mesh):
    return jax.shard_map(
        local,
        mesh=mesh,
        in_specs=(
            P("visit", "patch", None, None),
            P("visit", "patch", None, None),
            P("visit", None, None),
            P("visit", None),
            P("visit", None),
            P("visit", None, None),
            P("visit", None),
        ),
        out_specs=(P("visit", "patch"), P("visit", "patch")),
        check_vma=False,
    )
```

profile of v0, /device:TPU:5, one launch (start us, length us, event | category | flops | bytes accessed | tf_op | source)
XLA Modules:
  0.0 671.8 jit_solution(11030103022260496552)
XLA Ops:
  32.3 1.4 fusion.115
  38.0 1.4 fusion.112
  43.7 1.4 fusion.113
  49.4 1.4 fusion.114
  51.3 119.2 %while.28 = (s32[]{:T(128)}, bf16[6,128,512]{2,1,0:T(8,128)(2,1)S(1)}, f32[6,3,40]{2,1,0:T(4,128)S(1)}, bf16[6,128,512]{1,2,0:T(8,128)(2,1)S(1)}, bf16[4,4,128,1...) while((s32[]{:T(128)}, ...), condition=%wide.region_53.54_spmd.clone.clone, body=%wide.region_16.53_spmd.clone.clone.sunk | while | flops 2971667456 | bytes 70542368 | solution.py:123
  52.3 2.0 multiply_reduce_fusion.58
  54.4 1.7 multiply_reduce_fusion.59
  62.8 8.5 %fusion.219 = bf16[6,128,512]{2,1,0:T(8,128)(2,1)S(1)} fusion(bf16[6,128,512]{2,1,0:T(8,128)(2,1)S(1)} %get-tuple-element.857, s32[]{:T(128)} %get-tuple-element.856, bf16[4,4,512,512]{3,2,1,0:T(8,128)(2,1)S(1)} %copy-done, f32[128,512]{1,0:T(8,128)S(1)} %get-tuple-element.764, f32[128,512]{1,0:T(8,128)S(1)} %get-tuple-element.765, ...), kind=kOutput, calls=%fused_computation.133.clone.1 | convolution fusion | flops 73138176 | bytes 11012660 | tf_op jit(solution)/shard_map/while/body/eval_jaxpr/drw,xw->drx/dot_general | solution.py:52
  72.2 2.0 multiply_reduce_fusion.58
  74.2 1.7 multiply_reduce_fusion.59
  82.6 8.5 %fusion.219 = bf16[6,128,512]{2,1,0:T(8,128)(2,1)S(1)} fusion(bf16[6,128,512]{2,1,0:T(8,128)(2,1)S(1)} %get-tuple-element.857, s32[]{:T(128)} %get-tuple-element.856, bf16[4,4,512,512]{3,2,1,0:T(8,128)(2,1)S(1)} %copy-done, f32[128,512]{1,0:T(8,128)S(1)} %get-tuple-element.764, f32[128,512]{1,0:T(8,128)S(1)} %get-tuple-element.765, ...), kind=kOutput, calls=%fused_computation.133.clone.1 | convolution fusion | flops 73138176 | bytes 11012660 | tf_op jit(solution)/shard_map/while/body/eval_jaxpr/drw,xw->drx/dot_general | solution.py:52
  92.0 2.0 multiply_reduce_fusion.58
  94.1 1.7 multiply_reduce_fusion.59
  102.4 8.5 %fusion.219 = bf16[6,128,512]{2,1,0:T(8,128)(2,1)S(1)} fusion(bf16[6,128,512]{2,1,0:T(8,128)(2,1)S(1)} %get-tuple-element.857, s32[]{:T(128)} %get-tuple-element.856, bf16[4,4,512,512]{3,2,1,0:T(8,128)(2,1)S(1)} %copy-done, f32[128,512]{1,0:T(8,128)S(1)} %get-tuple-element.764, f32[128,512]{1,0:T(8,128)S(1)} %get-tuple-element.765, ...), kind=kOutput, calls=%fused_computation.133.clone.1 | convolution fusion | flops 73138176 | bytes 11012660 | tf_op jit(solution)/shard_map/while/body/eval_jaxpr/drw,xw->drx/dot_general | solution.py:52
  111.8 2.0 multiply_reduce_fusion.58
  113.9 1.7 multiply_reduce_fusion.59
  122.3 8.5 %fusion.219 = bf16[6,128,512]{2,1,0:T(8,128)(2,1)S(1)} fusion(bf16[6,128,512]{2,1,0:T(8,128)(2,1)S(1)} %get-tuple-element.857, s32[]{:T(128)} %get-tuple-element.856, bf16[4,4,512,512]{3,2,1,0:T(8,128)(2,1)S(1)} %copy-done, f32[128,512]{1,0:T(8,128)S(1)} %get-tuple-element.764, f32[128,512]{1,0:T(8,128)S(1)} %get-tuple-element.765, ...), kind=kOutput, calls=%fused_computation.133.clone.1 | convolution fusion | flops 73138176 | bytes 11012660 | tf_op jit(solution)/shard_map/while/body/eval_jaxpr/drw,xw->drx/dot_general | solution.py:52
  131.7 2.0 multiply_reduce_fusion.58
  133.7 1.7 multiply_reduce_fusion.59
  142.1 8.5 %fusion.219 = bf16[6,128,512]{2,1,0:T(8,128)(2,1)S(1)} fusion(bf16[6,128,512]{2,1,0:T(8,128)(2,1)S(1)} %get-tuple-element.857, s32[]{:T(128)} %get-tuple-element.856, bf16[4,4,512,512]{3,2,1,0:T(8,128)(2,1)S(1)} %copy-done, f32[128,512]{1,0:T(8,128)S(1)} %get-tuple-element.764, f32[128,512]{1,0:T(8,128)S(1)} %get-tuple-element.765, ...), kind=kOutput, calls=%fused_computation.133.clone.1 | convolution fusion | flops 73138176 | bytes 11012660 | tf_op jit(solution)/shard_map/while/body/eval_jaxpr/drw,xw->drx/dot_general | solution.py:52
  151.5 2.0 multiply_reduce_fusion.58
  153.6 1.7 multiply_reduce_fusion.59
  161.9 8.5 %fusion.219 = bf16[6,128,512]{2,1,0:T(8,128)(2,1)S(1)} fusion(bf16[6,128,512]{2,1,0:T(8,128)(2,1)S(1)} %get-tuple-element.857, s32[]{:T(128)} %get-tuple-element.856, bf16[4,4,512,512]{3,2,1,0:T(8,128)(2,1)S(1)} %copy-done, f32[128,512]{1,0:T(8,128)S(1)} %get-tuple-element.764, f32[128,512]{1,0:T(8,128)S(1)} %get-tuple-element.765, ...), kind=kOutput, calls=%fused_computation.133.clone.1 | convolution fusion | flops 73138176 | bytes 11012660 | tf_op jit(solution)/shard_map/while/body/eval_jaxpr/drw,xw->drx/dot_general | solution.py:52
  171.5 101.2 %all-gather.2.cloned.1.call-done = bf16[96,128,512]{2,1,0:T(8,128)(2,1)} async-done(((bf16[6,128,512]{2,1,0:T(8,128)(2,1)}), bf16[96,128,512]{2,1,0:T(8,128)(2,1)}) %all-gather.2.cloned.1.call-update) | async-done | bytes 12582928 | tf_op jit(solution)/shard_map/all_gather | solution.py:141
  272.8 335.8 %while.27 = (s32[]{:T(128)}, f32[128,512]{1,0:T(8,128)S(1)}, f32[128,512]{1,0:T(8,128)S(1)}, s32[96,2]{0,1:T(2,128)S(1)}, s32[]{:T(128)}, /*index=5*/f32[96]{0:T...) while((s32[]{:T(128)}, f32[128,512]{1,0:T(8,128)S(1)}, ...), condition=%wide.region_59.60_spmd, body=%wide.region_54.59_spmd.sunk | while | flops 88949520 | bytes 1204658 | solution.py:153
  282.8 9.6 %conditional.2 = ((f32[128,512]{1,0:T(8,128)S(1)}, f32[128,512]{1,0:T(8,128)S(1)})) conditional(s32[]{:T(128)} %convert_element_type.1283, (f32[128,512]{1,0:T(8,128)S(1)}, f32[128,512]{1,0:T(8,128)S(1)}) %tuple.161, (s32[]{:T(128)}, f32[96]{0:T(128)S(1)}, s32[96]{0:T(128)S(1)}, f32[96,2]{0,1:T(2,128)S(1)}, bf16[96,128,512]{2,1,0:T(8,128)(2,1)}, ...), branch_computations={%region_55.55_spmd, %region_56.58_spmd} | conditional | flops 88949512 | bytes 1204415 | solution.py:147
  290.5 1.9 fusion.4
  318.3 9.6 %conditional.2 = ((f32[128,512]{1,0:T(8,128)S(1)}, f32[128,512]{1,0:T(8,128)S(1)})) conditional(s32[]{:T(128)} %convert_element_type.1283, (f32[128,512]{1,0:T(8,128)S(1)}, f32[128,512]{1,0:T(8,128)S(1)}) %tuple.161, (s32[]{:T(128)}, f32[96]{0:T(128)S(1)}, s32[96]{0:T(128)S(1)}, f32[96,2]{0,1:T(2,128)S(1)}, bf16[96,128,512]{2,1,0:T(8,128)(2,1)}, ...), branch_computations={%region_55.55_spmd, %region_56.58_spmd} | conditional | flops 88949512 | bytes 1204415 | solution.py:147
  326.0 1.9 fusion.4
  337.9 9.6 %conditional.2 = ((f32[128,512]{1,0:T(8,128)S(1)}, f32[128,512]{1,0:T(8,128)S(1)})) conditional(s32[]{:T(128)} %convert_element_type.1283, (f32[128,512]{1,0:T(8,128)S(1)}, f32[128,512]{1,0:T(8,128)S(1)}) %tuple.161, (s32[]{:T(128)}, f32[96]{0:T(128)S(1)}, s32[96]{0:T(128)S(1)}, f32[96,2]{0,1:T(2,128)S(1)}, bf16[96,128,512]{2,1,0:T(8,128)(2,1)}, ...), branch_computations={%region_55.55_spmd, %region_56.58_spmd} | conditional | flops 88949512 | bytes 1204415 | solution.py:147
  345.6 1.9 fusion.4
  357.5 9.6 %conditional.2 = ((f32[128,512]{1,0:T(8,128)S(1)}, f32[128,512]{1,0:T(8,128)S(1)})) conditional(s32[]{:T(128)} %convert_element_type.1283, (f32[128,512]{1,0:T(8,128)S(1)}, f32[128,512]{1,0:T(8,128)S(1)}) %tuple.161, (s32[]{:T(128)}, f32[96]{0:T(128)S(1)}, s32[96]{0:T(128)S(1)}, f32[96,2]{0,1:T(2,128)S(1)}, bf16[96,128,512]{2,1,0:T(8,128)(2,1)}, ...), branch_computations={%region_55.55_spmd, %region_56.58_spmd} | conditional | flops 88949512 | bytes 1204415 | solution.py:147
  365.2 1.9 fusion.4
  377.1 9.6 %conditional.2 = ((f32[128,512]{1,0:T(8,128)S(1)}, f32[128,512]{1,0:T(8,128)S(1)})) conditional(s32[]{:T(128)} %convert_element_type.1283, (f32[128,512]{1,0:T(8,128)S(1)}, f32[128,512]{1,0:T(8,128)S(1)}) %tuple.161, (s32[]{:T(128)}, f32[96]{0:T(128)S(1)}, s32[96]{0:T(128)S(1)}, f32[96,2]{0,1:T(2,128)S(1)}, bf16[96,128,512]{2,1,0:T(8,128)(2,1)}, ...), branch_computations={%region_55.55_spmd, %region_56.58_spmd} | conditional | flops 88949512 | bytes 1204415 | solution.py:147
  384.8 1.9 fusion.4
  394.7 9.6 %conditional.2 = ((f32[128,512]{1,0:T(8,128)S(1)}, f32[128,512]{1,0:T(8,128)S(1)})) conditional(s32[]{:T(128)} %convert_element_type.1283, (f32[128,512]{1,0:T(8,128)S(1)}, f32[128,512]{1,0:T(8,128)S(1)}) %tuple.161, (s32[]{:T(128)}, f32[96]{0:T(128)S(1)}, s32[96]{0:T(128)S(1)}, f32[96,2]{0,1:T(2,128)S(1)}, bf16[96,128,512]{2,1,0:T(8,128)(2,1)}, ...), branch_computations={%region_55.55_spmd, %region_56.58_spmd} | conditional | flops 88949512 | bytes 1204415 | solution.py:147
  402.4 1.9 fusion.4
  416.3 9.6 %conditional.2 = ((f32[128,512]{1,0:T(8,128)S(1)}, f32[128,512]{1,0:T(8,128)S(1)})) conditional(s32[]{:T(128)} %convert_element_type.1283, (f32[128,512]{1,0:T(8,128)S(1)}, f32[128,512]{1,0:T(8,128)S(1)}) %tuple.161, (s32[]{:T(128)}, f32[96]{0:T(128)S(1)}, s32[96]{0:T(128)S(1)}, f32[96,2]{0,1:T(2,128)S(1)}, bf16[96,128,512]{2,1,0:T(8,128)(2,1)}, ...), branch_computations={%region_55.55_spmd, %region_56.58_spmd} | conditional | flops 88949512 | bytes 1204415 | solution.py:147
  424.0 1.9 fusion.4
  437.9 9.6 %conditional.2 = ((f32[128,512]{1,0:T(8,128)S(1)}, f32[128,512]{1,0:T(8,128)S(1)})) conditional(s32[]{:T(128)} %convert_element_type.1283, (f32[128,512]{1,0:T(8,128)S(1)}, f32[128,512]{1,0:T(8,128)S(1)}) %tuple.161, (s32[]{:T(128)}, f32[96]{0:T(128)S(1)}, s32[96]{0:T(128)S(1)}, f32[96,2]{0,1:T(2,128)S(1)}, bf16[96,128,512]{2,1,0:T(8,128)(2,1)}, ...), branch_computations={%region_55.55_spmd, %region_56.58_spmd} | conditional | flops 88949512 | bytes 1204415 | solution.py:147
  445.6 1.9 fusion.4
  465.4 9.6 %conditional.2 = ((f32[128,512]{1,0:T(8,128)S(1)}, f32[128,512]{1,0:T(8,128)S(1)})) conditional(s32[]{:T(128)} %convert_element_type.1283, (f32[128,512]{1,0:T(8,128)S(1)}, f32[128,512]{1,0:T(8,128)S(1)}) %tuple.161, (s32[]{:T(128)}, f32[96]{0:T(128)S(1)}, s32[96]{0:T(128)S(1)}, f32[96,2]{0,1:T(2,128)S(1)}, bf16[96,128,512]{2,1,0:T(8,128)(2,1)}, ...), branch_computations={%region_55.55_spmd, %region_56.58_spmd} | conditional | flops 88949512 | bytes 1204415 | solution.py:147
  473.2 1.9 fusion.4
  487.0 9.6 %conditional.2 = ((f32[128,512]{1,0:T(8,128)S(1)}, f32[128,512]{1,0:T(8,128)S(1)})) conditional(s32[]{:T(128)} %convert_element_type.1283, (f32[128,512]{1,0:T(8,128)S(1)}, f32[128,512]{1,0:T(8,128)S(1)}) %tuple.161, (s32[]{:T(128)}, f32[96]{0:T(128)S(1)}, s32[96]{0:T(128)S(1)}, f32[96,2]{0,1:T(2,128)S(1)}, bf16[96,128,512]{2,1,0:T(8,128)(2,1)}, ...), branch_computations={%region_55.55_spmd, %region_56.58_spmd} | conditional | flops 88949512 | bytes 1204415 | solution.py:147
  494.7 1.9 fusion.4
  512.6 9.6 %conditional.2 = ((f32[128,512]{1,0:T(8,128)S(1)}, f32[128,512]{1,0:T(8,128)S(1)})) conditional(s32[]{:T(128)} %convert_element_type.1283, (f32[128,512]{1,0:T(8,128)S(1)}, f32[128,512]{1,0:T(8,128)S(1)}) %tuple.161, (s32[]{:T(128)}, f32[96]{0:T(128)S(1)}, s32[96]{0:T(128)S(1)}, f32[96,2]{0,1:T(2,128)S(1)}, bf16[96,128,512]{2,1,0:T(8,128)(2,1)}, ...), branch_computations={%region_55.55_spmd, %region_56.58_spmd} | conditional | flops 88949512 | bytes 1204415 | solution.py:147
  520.3 1.9 fusion.4
  528.2 9.6 %conditional.2 = ((f32[128,512]{1,0:T(8,128)S(1)}, f32[128,512]{1,0:T(8,128)S(1)})) conditional(s32[]{:T(128)} %convert_element_type.1283, (f32[128,512]{1,0:T(8,128)S(1)}, f32[128,512]{1,0:T(8,128)S(1)}) %tuple.161, (s32[]{:T(128)}, f32[96]{0:T(128)S(1)}, s32[96]{0:T(128)S(1)}, f32[96,2]{0,1:T(2,128)S(1)}, bf16[96,128,512]{2,1,0:T(8,128)(2,1)}, ...), branch_computations={%region_55.55_spmd, %region_56.58_spmd} | conditional | flops 88949512 | bytes 1204415 | solution.py:147
  535.9 1.9 fusion.4
  553.8 9.6 %conditional.2 = ((f32[128,512]{1,0:T(8,128)S(1)}, f32[128,512]{1,0:T(8,128)S(1)})) conditional(s32[]{:T(128)} %convert_element_type.1283, (f32[128,512]{1,0:T(8,128)S(1)}, f32[128,512]{1,0:T(8,128)S(1)}) %tuple.161, (s32[]{:T(128)}, f32[96]{0:T(128)S(1)}, s32[96]{0:T(128)S(1)}, f32[96,2]{0,1:T(2,128)S(1)}, bf16[96,128,512]{2,1,0:T(8,128)(2,1)}, ...), branch_computations={%region_55.55_spmd, %region_56.58_spmd} | conditional | flops 88949512 | bytes 1204415 | solution.py:147
  561.5 1.9 fusion.4
  569.4 9.6 %conditional.2 = ((f32[128,512]{1,0:T(8,128)S(1)}, f32[128,512]{1,0:T(8,128)S(1)})) conditional(s32[]{:T(128)} %convert_element_type.1283, (f32[128,512]{1,0:T(8,128)S(1)}, f32[128,512]{1,0:T(8,128)S(1)}) %tuple.161, (s32[]{:T(128)}, f32[96]{0:T(128)S(1)}, s32[96]{0:T(128)S(1)}, f32[96,2]{0,1:T(2,128)S(1)}, bf16[96,128,512]{2,1,0:T(8,128)(2,1)}, ...), branch_computations={%region_55.55_spmd, %region_56.58_spmd} | conditional | flops 88949512 | bytes 1204415 | solution.py:147
  577.1 1.9 fusion.4
  595.0 9.6 %conditional.2 = ((f32[128,512]{1,0:T(8,128)S(1)}, f32[128,512]{1,0:T(8,128)S(1)})) conditional(s32[]{:T(128)} %convert_element_type.1283, (f32[128,512]{1,0:T(8,128)S(1)}, f32[128,512]{1,0:T(8,128)S(1)}) %tuple.161, (s32[]{:T(128)}, f32[96]{0:T(128)S(1)}, s32[96]{0:T(128)S(1)}, f32[96,2]{0,1:T(2,128)S(1)}, bf16[96,128,512]{2,1,0:T(8,128)(2,1)}, ...), branch_computations={%region_55.55_spmd, %region_56.58_spmd} | conditional | flops 88949512 | bytes 1204415 | solution.py:147
  602.7 1.9 fusion.4
  611.4 8.4 %reduce-scatter.3.cloned.1.call-done = f32[64,512]{1,0:T(8,128)} async-done(((f32[128,512]{1,0:T(8,128)}), f32[64,512]{1,0:T(8,128)}) %reduce-scatter.3.cloned.1.call-update) | async-done | bytes 131088 | tf_op jit(solution)/shard_map/reduce_scatter | solution.py:155
  619.7 14.0 %reduce-scatter.5.cloned.1.call-done = f32[64,512]{1,0:T(8,128)} async-done(((f32[128,512]{1,0:T(8,128)}), f32[64,512]{1,0:T(8,128)}) %reduce-scatter.5.cloned.1.call-update) | async-done | bytes 131088 | tf_op jit(solution)/shard_map/reduce_scatter | solution.py:156
  634.8 2.2 collective-permute-start
  638.3 3.1 collective-permute-done.1
  641.4 5.3 collective-permute-start.2
  646.7 1.9 collective-permute-start.3
  649.3 3.6 collective-permute-done.3
  653.0 5.7 fusion.128
  658.7 6.5 fusion.136
  (552 shorter events, 202.2 us)
Async XLA Ops:
  7.2 43.7 %copy-start.4 = (bf16[1,6,128,512]{3,2,1,0:T(8,128)(2,1)S(1)}, bf16[1,6,128,512]{3,2,1,0:T(8,128)(2,1)}, u32[]{:S(2)}) copy-start(bf16[1,6,128,512]{3,2,1,0:T(8,128)(2,1)} %param.13) | copy-start | bytes 2359300
  7.2 44.1 %copy-start.8 = (f32[1,6,3,40]{3,0,2,1:T(1,128)S(1)}, f32[1,6,3,40]{3,0,2,1:T(1,128)}, u32[]{:S(2)}) copy-start(f32[1,6,3,40]{3,0,2,1:T(1,128)} %param.14) | copy-start | bytes 8644
  7.2 265.5 %all-gather.2.cloned.1.call-start = ((), (), s32[]{:S(2)}) async-start(), calls=%async_computation.2 | async-start | bytes 13369344 | tf_op jit(solution)/shard_map/all_gather | solution.py:141
  51.3 221.5 %copy-start.6 = (s32[1,96,2]{1,2,0:T(2,128)S(1)}, s32[1,96,2]{1,2,0:T(2,128)}, u32[]{:S(2)}) copy-start(s32[1,96,2]{1,2,0:T(2,128)} %param.15) | copy-start | bytes 2308
  51.3 221.5 %copy-start.7 = (f32[1,96,2]{1,2,0:T(2,128)S(1)}, f32[1,96,2]{1,2,0:T(2,128)}, u32[]{:S(2)}) copy-start(f32[1,96,2]{1,2,0:T(2,128)} %param.18) | copy-start | bytes 2308
  51.3 221.5 %copy-start.9 = (f32[1,96]{1,0:T(1,128)S(1)}, f32[1,96]{1,0:T(1,128)}, u32[]{:S(2)}) copy-start(f32[1,96]{1,0:T(1,128)} %param.19) | copy-start | bytes 1156
  51.3 221.5 %copy-start.10 = (s32[1,96]{1,0:T(1,128)S(1)}, s32[1,96]{1,0:T(1,128)}, u32[]{:S(2)}) copy-start(s32[1,96]{1,0:T(1,128)} %param.16) | copy-start | bytes 1156
  51.3 221.5 %copy-start.11 = (s32[1,96]{1,0:T(1,128)S(1)}, s32[1,96]{1,0:T(1,128)}, u32[]{:S(2)}) copy-start(s32[1,96]{1,0:T(1,128)} %param.17) | copy-start | bytes 1156
  51.5 4.7 copy-start
  71.3 4.7 copy-start
  91.2 4.7 copy-start
  111.0 4.7 copy-start
  130.8 4.7 copy-start
  150.7 4.7 copy-start
  170.5 0.9 copy-start.5
  171.4 448.3 %reduce-scatter.3.cloned.1.call-start = ((), (), s32[]{:S(2)}) async-start(), calls=%async_computation.3 | async-start | bytes 393216 | tf_op jit(solution)/shard_map/reduce_scatter | solution.py:155
  608.6 0.7 copy-start.3
  608.6 0.8 copy-start.1
  609.3 24.4 %reduce-scatter.5.cloned.1.call-start = ((), (), s32[]{:S(2)}) async-start(), calls=%async_computation.4 | async-start | bytes 393216 | tf_op jit(solution)/shard_map/reduce_scatter | solution.py:156
  634.7 30.5 %copy-start.2 = (f32[64,512]{1,0:T(8,128)}, f32[64,512]{1,0:T(8,128)S(1)}, u32[]{:S(2)}) copy-start(f32[64,512]{1,0:T(8,128)S(1)} %maximum_divide_fusion) | copy-start | bytes 393220
  634.8 3.5 collective-permute-start
  636.9 4.4 collective-permute-start.1
  641.4 7.9 %collective-permute-start.2 = (f32[72,4]{1,0:T(8,128)S(1)}, f32[72,4]{1,0:T(8,128)S(1)}, u32[]{:S(2)}, u32[]{:S(2)}) collective-permute-start(f32[72,4]{1,0:T(8,128)S(1)} %get-tuple-element.558), channel_id=1, source_target_pairs={{0,1},{1,2},{2,3},{3,4},{4,5},{5,6},{6,7},{7,8},{8,9},{9,10},{10,1... | collective-permute-start | bytes 3464 | tf_op jit(solution)/shard_map/ppermute | solution.py:18
  646.7 6.2 collective-permute-start.3
Sparse Core Ops, SparseCore 0:
  171.6 101.1 all-gather.1
  609.4 10.2 reduce-scatter.2
  622.0 11.7 reduce-scatter.4
where the time goes:
time: 676 us; the launch traced here: 672 us
  loops' own time  185 us (27%)
  matrix products  141 us (21%)
  waiting for transfers between devices  131 us (19%)
  local copies, waits for them, and re-layouts  107 us (16%)
  other arithmetic  71.6 us (11%)
  between operations  25.4 us (4%)
  starting transfers between devices  10.8 us (2%)
    another operation x1, loops' own time, local(): flux_sum, cover_sum = lax.fori_loop(0, arrived.shape[0], visit_one, empty)  128 us
    dot_general x96, matrix products, match_exposure(): jnp.einsum('drw,xw->drx', smoothed[group, :count], col_band[group, x_degr...  108 us
    all_gather x1, waiting for transfers between devices, local(): arrived = lax.all_gather(matched, 'patch', axis=0, tiled=True)  101 us
    dynamic_slice x96, local copies, waits for them, and re-layouts, visit_one(): hit_second = table[offset, 1] == own_patch  62.7 us
    another operation x96, loops' own time, visit_one(): lax.cond(hit_first | hit_second, lambda: add_exposure(inner, exposure, of...  56 us
    dot_general x15, matrix products, warp_exposure(): warped = jnp.dot(middle, col_map, preferred_element_type=jnp.float32)  28.8 us
    unnamed x30, other arithmetic  21.1 us
    reduce_scatter x1, waiting for transfers between devices, local(): lax.psum_scatter(cover_sum, 'visit', scatter_dimension=0, tiled=True)  14 us
  transfers between devices with their start and end apart: 7, of which 5 were waited for; matrix products, arithmetic and copies ran while one was open for 0% of the time, Pallas kernels for 0%

commit v1 on v0

--- a/solution.py
+++ b/solution.py
@@ -6,6 +6,18 @@
 KRAD = 10
 DRAD = 4
 WIDTHS_PX = (1.0, 1.7, 2.6, 3.6)
+
+
+def doubled_up(array, axis, dim):
+    ways, here, step = (lax.axis_size(axis), lax.axis_index(axis), array.shape[dim])
+    line, have = (array, 1)
+    while have < ways:
+        line = jnp.concatenate(
+            [line, lax.ppermute(line, axis, [(d, (d - have) % ways) for d in range(ways)])],
+            axis=dim,
+        )
+        have = 2 * have
+    return jnp.roll(line, here * step, axis=dim)
 
 
 def extended(array, sides, width):
@@ -138,7 +150,7 @@
         )
         return (totals[0] + flux_part, totals[1] + cover_part)
 
-    arrived = lax.all_gather(matched, "patch", axis=0, tiled=True)
+    arrived = doubled_up(matched, "patch", 0)
 
     def visit_one(offset, inner):
         hit_first = table[offset, 0] == own_patch

time: 676 us -> 992 us (1.47)
  waiting for transfers between devices: 131 us -> 405 us
  local copies, waits for them, and re-layouts: 107 us -> 140 us
  loops' own time: 185 us -> 175 us
    ppermute x0 -> x4, waiting for transfers between devices: none -> 376 us  [doubled_up(): lax.ppermute(line, axis, [(d, (d - have) % ways) for d in range(ways)])]
    all_gather x1 -> x0, waiting for transfers between devices: 101 us -> none  [local(): arrived = lax.all_gather(matched, 'patch', axis=0, tiled=True)]
    unnamed x24 -> x43, local copies, waits for them, and re-layouts: 2.04 us -> 21.4 us
    dynamic_slice x0 -> x1, local copies, waits for them, and re-layouts: none -> 10.7 us  [doubled_up(): return jnp.roll(line, here * step, axis=dim)]
  transfers between devices with their start and end apart: 7 -> 10, of which waited for: 5 -> 8; matrix products, arithmetic and copies ran while one was open for 0% -> 1% of each run, Pallas kernels for 0% -> 0%
where the time goes in v1:
time: 992 us; the launch traced here: 981 us
  waiting for transfers between devices  405 us (41%)
  loops' own time  175 us (18%)
  matrix products  141 us (14%)
  local copies, waits for them, and re-layouts  140 us (14%)
  other arithmetic  77 us (8%)
  between operations  25.7 us (3%)
  starting transfers between devices  17.6 us (2%)
    ppermute x4, waiting for transfers between devices, doubled_up(): lax.ppermute(line, axis, [(d, (d - have) % ways) for d in range(ways)])  376 us
    another operation x1, loops' own time, local(): flux_sum, cover_sum = lax.fori_loop(0, arrived.shape[0], visit_one, empty)  118 us
    dot_general x96, matrix products, match_exposure(): jnp.einsum('drw,xw->drx', smoothed[group, :count], col_band[group, x_degr...  108 us
    dynamic_slice x96, local copies, waits for them, and re-layouts, visit_one(): hit_second = table[offset, 1] == own_patch  59.1 us
    another operation x96, loops' own time, visit_one(): lax.cond(hit_first | hit_second, lambda: add_exposure(inner, exposure, of...  56.2 us
    dot_general x15, matrix products, warp_exposure(): warped = jnp.dot(middle, col_map, preferred_element_type=jnp.float32)  29 us
    unnamed x43, local copies, waits for them, and re-layouts  21.4 us
    unnamed x30, other arithmetic  21.1 us
  transfers between devices with their start and end apart: 10, of which 8 were waited for; matrix products, arithmetic and copies ran while one was open for 1% of the time, Pallas kernels for 0%

profile of v1, /device:TPU:5, one launch (start us, length us, event | category | flops | bytes accessed | tf_op | source)
XLA Modules:
  0.0 981.5 jit_solution(7296078706080223551)
XLA Ops:
  51.2 119.1 %while.28 = (s32[]{:T(128)}, bf16[6,128,512]{2,1,0:T(8,128)(2,1)S(1)}, f32[6,3,40]{2,1,0:T(4,128)S(1)}, bf16[6,128,512]{1,2,0:T(8,128)(2,1)S(1)}, bf16[4,4,128,1...) while((s32[]{:T(128)}, ...), condition=%wide.region_53.54_spmd.clone.clone, body=%wide.region_16.53_spmd.clone.clone.sunk | while | flops 2971667456 | bytes 70542368 | solution.py:135
  52.3 2.0 multiply_reduce_fusion.58
  62.7 8.5 fusion.219
  72.1 2.0 multiply_reduce_fusion.58
  82.5 8.5 fusion.219
  91.9 2.0 multiply_reduce_fusion.58
  102.4 8.5 fusion.219
  111.7 2.0 multiply_reduce_fusion.58
  122.2 8.5 fusion.219
  131.6 2.0 multiply_reduce_fusion.58
  142.0 8.5 fusion.219
  151.4 2.0 multiply_reduce_fusion.58
  161.8 8.5 fusion.219
  171.1 11.6 %collective-permute-done = bf16[6,128,512]{2,1,0:T(8,128)(2,1)S(1)} collective-permute-done((bf16[6,128,512]{2,1,0:T(8,128)(2,1)S(1)}, bf16[6,128,512]{2,1,0:T(8,128)(2,1)S(1)}, u32[]{:S(2)}, u32[]{:S(2)}) %collective-permute-start) | collective-permute-done | bytes 786464 | tf_op jit(solution)/shard_map/ppermute | solution.py:16
  183.0 35.3 %collective-permute-done.1 = bf16[12,128,512]{2,1,0:T(8,128)(2,1)S(1)} collective-permute-done((bf16[12,128,512]{2,1,0:T(8,128)(2,1)S(1)}, bf16[12,128,512]{2,1,0:T(8,128)(2,1)S(1)}, u32[]{:S(2)}, u32[]{:S(2)}) %collective-permute-start.1) | collective-permute-done | bytes 1572896 | tf_op jit(solution)/shard_map/ppermute | solution.py:16
  218.6 5.2 collective-permute-start.2
  223.8 65.6 %collective-permute-done.2 = bf16[24,128,512]{2,1,0:T(8,128)(2,1)S(1)} collective-permute-done((bf16[24,128,512]{2,1,0:T(8,128)(2,1)S(1)}, bf16[24,128,512]{2,1,0:T(8,128)(2,1)S(1)}, u32[]{:S(2)}, u32[]{:S(2)}) %collective-permute-start.2) | collective-permute-done | bytes 3145760 | tf_op jit(solution)/shard_map/ppermute | solution.py:16
  289.4 4.5 pad_maximum_fusion
  294.8 2.1 constant_dynamic-update-slice_fusion.25
  296.9 2.1 constant_dynamic-update-slice_fusion.24
  299.0 2.7 constant_dynamic-update-slice_fusion.23
  301.7 2.0 constant_dynamic-update-slice_fusion.22
  303.7 263.2 %collective-permute-done.3 = bf16[48,128,512]{2,1,0:T(8,128)(2,1)} collective-permute-done((bf16[48,128,512]{2,1,0:T(8,128)(2,1)}, bf16[48,128,512]{2,1,0:T(8,128)(2,1)}, u32[]{:S(2)}, u32[]{:S(2)}) %collective-permute-start.3) | collective-permute-done | bytes 6291488 | tf_op jit(solution)/shard_map/ppermute | solution.py:16
  566.9 6.1 constant_dynamic-update-slice_fusion.21
  576.4 1.9 constant_dynamic-update-slice_fusion.17
  578.3 6.1 constant_dynamic-update-slice_fusion.16
  584.4 10.7 %constant_dynamic-slice_fusion.4 = bf16[96,128,512]{2,1,0:T(8,128)(2,1)} fusion(bf16[192,128,512]{2,1,0:T(8,128)(2,1)} %constant_dynamic-update-slice_fusion.16, s32[]{:T(128)S(6)} %select_n.407), kind=kLoop, calls=%fused_computation.423 | loop fusion | bytes 25165828 | tf_op jit(solution)/shard_map/jit(_roll_dynamic)/dynamic_slice | solution.py:20
  595.2 323.2 %while.27 = (s32[]{:T(128)}, f32[128,512]{1,0:T(8,128)S(1)}, f32[128,512]{1,0:T(8,128)S(1)}, s32[96,2]{0,1:T(2,128)S(1)}, s32[]{:T(128)}, /*index=5*/f32[96]{0:T...) while((s32[]{:T(128)}, f32[128,512]{1,0:T(8,128)S(1)}, ...), condition=%wide.region_59.60_spmd, body=%wide.region_54.59_spmd.sunk | while | flops 88949520 | bytes 1204658 | solution.py:165
  604.4 9.7 conditional.2
  612.2 1.9 fusion.4
  638.2 9.7 conditional.2
  645.9 1.9 fusion.4
  657.1 9.7 conditional.2
  676.1 9.7 conditional.2
  683.8 1.9 fusion.4
  695.0 9.7 conditional.2
  702.8 1.9 fusion.4
  712.1 9.7 conditional.2
  719.9 1.9 fusion.4
  732.9 9.7 conditional.2
  740.7 1.9 fusion.4
  753.7 9.7 conditional.2
  761.5 1.9 fusion.4
  780.1 9.7 conditional.2
  787.9 1.9 fusion.4
  800.9 9.7 conditional.2
  825.4 9.7 conditional.2
  833.2 1.9 fusion.4
  840.7 9.7 conditional.2
  848.4 1.9 fusion.4
  865.2 9.7 conditional.2
  872.9 1.9 fusion.4
  880.4 9.7 conditional.2
  888.2 1.9 fusion.4
  904.9 9.7 conditional.2
  912.7 1.9 fusion.4
  921.1 8.0 reduce-scatter.3.cloned.1.call-done
  929.1 14.0 %reduce-scatter.5.cloned.1.call-done = f32[64,512]{1,0:T(8,128)} async-done(((f32[128,512]{1,0:T(8,128)}), f32[64,512]{1,0:T(8,128)}) %reduce-scatter.5.cloned.1.call-update) | async-done | bytes 131088 | tf_op jit(solution)/shard_map/reduce_scatter | solution.py:168
  944.2 2.2 collective-permute-start.4
  947.7 3.1 collective-permute-done.5
  950.8 5.2 collective-permute-start.6
  958.7 3.6 collective-permute-done.7
  962.4 5.7 fusion.128
  968.1 6.5 fusion.136
  (581 shorter events, 225.5 us)
Async XLA Ops:
  7.2 43.7 %copy-start.10 = (bf16[1,6,128,512]{3,2,1,0:T(8,128)(2,1)S(1)}, bf16[1,6,128,512]{3,2,1,0:T(8,128)(2,1)}, u32[]{:S(2)}) copy-start(bf16[1,6,128,512]{3,2,1,0:T(8,128)(2,1)} %param.13) | copy-start | bytes 2359300
  7.2 44.1 %copy-start.13 = (f32[1,6,3,40]{3,0,2,1:T(1,128)S(1)}, f32[1,6,3,40]{3,0,2,1:T(1,128)}, u32[]{:S(2)}) copy-start(f32[1,6,3,40]{3,0,2,1:T(1,128)} %param.14) | copy-start | bytes 8644
  7.2 921.9 %reduce-scatter.3.cloned.1.call-start = ((), (), s32[]{:S(2)}) async-start(), calls=%async_computation.2 | async-start | bytes 393216 | tf_op jit(solution)/shard_map/reduce_scatter | solution.py:167
  51.4 4.7 copy-start.6
  71.3 4.7 copy-start.6
  91.1 4.7 copy-start.6
  110.9 4.7 copy-start.6
  130.7 4.7 copy-start.6
  150.6 4.7 copy-start.6
  170.4 47.9 %copy-start.2 = (bf16[6,128,512]{2,1,0:T(8,128)(2,1)}, bf16[6,128,512]{2,1,0:T(8,128)(2,1)S(1)}, u32[]{:S(2)}) copy-start(bf16[6,128,512]{2,1,0:T(8,128)(2,1)S(1)} %get-tuple-element.365) | copy-start | bytes 2359300
  170.4 12.4 %collective-permute-start = (bf16[6,128,512]{2,1,0:T(8,128)(2,1)S(1)}, bf16[6,128,512]{2,1,0:T(8,128)(2,1)S(1)}, u32[]{:S(2)}, u32[]{:S(2)}) collective-permute-start(bf16[6,128,512]{2,1,0:T(8,128)(2,1)S(1)} %get-tuple-element.365), channel_id=1, source_target_pairs={{0,15},{1,0},{2,1},{3,2},{4,3},{5,4},{6,5},{7,6},{8,7},{9,8},{10,9... | collective-permute-start | bytes 2359304 | tf_op jit(solution)/shard_map/ppermute | solution.py:16
  182.8 111.2 %copy-start.4 = (bf16[6,128,512]{2,1,0:T(8,128)(2,1)}, bf16[6,128,512]{2,1,0:T(8,128)(2,1)S(1)}, u32[]{:S(2)}) copy-start(bf16[6,128,512]{2,1,0:T(8,128)(2,1)S(1)} %collective-permute-done) | copy-start | bytes 2359300
  182.9 35.4 %collective-permute-start.1 = (bf16[12,128,512]{2,1,0:T(8,128)(2,1)S(1)}, bf16[12,128,512]{2,1,0:T(8,128)(2,1)S(1)}, u32[]{:S(2)}, u32[]{:S(2)}) collective-permute-start(bf16[12,128,512]{2,1,0:T(8,128)(2,1)S(1)} %pad_maximum_fusion.2), channel_id=1, source_target_pairs={{0,14},{1,15},{2,0},{3,1},{4,2},{5,3},{6,4},{7,5},{8,6},{9,7},{10,... | collective-permute-start | bytes 4718600 | tf_op jit(solution)/shard_map/ppermute | solution.py:16
  218.3 75.6 %copy-start = (bf16[12,128,512]{2,1,0:T(8,128)(2,1)}, bf16[12,128,512]{2,1,0:T(8,128)(2,1)S(1)}, u32[]{:S(2)}) copy-start(bf16[12,128,512]{2,1,0:T(8,128)(2,1)S(1)} %collective-permute-done.1) | copy-start | bytes 4718596
  218.6 70.8 %collective-permute-start.2 = (bf16[24,128,512]{2,1,0:T(8,128)(2,1)S(1)}, bf16[24,128,512]{2,1,0:T(8,128)(2,1)S(1)}, u32[]{:S(2)}, u32[]{:S(2)}) collective-permute-start(bf16[24,128,512]{2,1,0:T(8,128)(2,1)S(1)} %pad_maximum_fusion.1), channel_id=1, source_target_pairs={{0,12},{1,13},{2,14},{3,15},{4,0},{5,1},{6,2},{7,3},{8,4},{9,5},{1... | collective-permute-start | bytes 9437192 | tf_op jit(solution)/shard_map/ppermute | solution.py:16
  293.9 273.0 %collective-permute-start.3 = (bf16[48,128,512]{2,1,0:T(8,128)(2,1)}, bf16[48,128,512]{2,1,0:T(8,128)(2,1)}, u32[]{:S(2)}, u32[]{:S(2)}) collective-permute-start(bf16[48,128,512]{2,1,0:T(8,128)(2,1)} %pad_maximum_fusion), channel_id=1, source_target_pairs={{0,8},{1,9},{2,10},{3,11},{4,12},{5,13},{6,14},{7,15},{8,0},{9,1},... | collective-permute-start | bytes 18874376 | tf_op jit(solution)/shard_map/ppermute | solution.py:16
  301.7 271.3 %copy-start.3 = (bf16[6,128,512]{2,1,0:T(8,128)(2,1)S(1)}, bf16[6,128,512]{2,1,0:T(8,128)(2,1)}, u32[]{:S(2)}) copy-start(bf16[6,128,512]{2,1,0:T(8,128)(2,1)} %copy-done.2) | copy-start | bytes 2359300
  303.7 270.4 %copy-start.5 = (bf16[6,128,512]{2,1,0:T(8,128)(2,1)S(1)}, bf16[6,128,512]{2,1,0:T(8,128)(2,1)}, u32[]{:S(2)}) copy-start(bf16[6,128,512]{2,1,0:T(8,128)(2,1)} %copy-done.4) | copy-start | bytes 2359300
  303.7 271.3 %copy-start.1 = (bf16[12,128,512]{2,1,0:T(8,128)(2,1)S(1)}, bf16[12,128,512]{2,1,0:T(8,128)(2,1)}, u32[]{:S(2)}) copy-start(bf16[12,128,512]{2,1,0:T(8,128)(2,1)} %copy-done) | copy-start | bytes 4718596
  584.4 10.7 %copy-start.11 = (s32[1,96,2]{1,2,0:T(2,128)S(1)}, s32[1,96,2]{1,2,0:T(2,128)}, u32[]{:S(2)}) copy-start(s32[1,96,2]{1,2,0:T(2,128)} %param.15) | copy-start | bytes 2308
  584.4 10.7 %copy-start.12 = (f32[1,96,2]{1,2,0:T(2,128)S(1)}, f32[1,96,2]{1,2,0:T(2,128)}, u32[]{:S(2)}) copy-start(f32[1,96,2]{1,2,0:T(2,128)} %param.18) | copy-start | bytes 2308
  584.4 10.7 %copy-start.14 = (f32[1,96]{1,0:T(1,128)S(1)}, f32[1,96]{1,0:T(1,128)}, u32[]{:S(2)}) copy-start(f32[1,96]{1,0:T(1,128)} %param.19) | copy-start | bytes 1156
  584.4 10.8 %copy-start.15 = (s32[1,96]{1,0:T(1,128)S(1)}, s32[1,96]{1,0:T(1,128)}, u32[]{:S(2)}) copy-start(s32[1,96]{1,0:T(1,128)} %param.16) | copy-start | bytes 1156
  584.4 10.8 %copy-start.16 = (s32[1,96]{1,0:T(1,128)S(1)}, s32[1,96]{1,0:T(1,128)}, u32[]{:S(2)}) copy-start(s32[1,96]{1,0:T(1,128)} %param.17) | copy-start | bytes 1156
  918.3 0.7 copy-start.9
  918.3 0.8 copy-start.7
  919.1 24.1 %reduce-scatter.5.cloned.1.call-start = ((), (), s32[]{:S(2)}) async-start(), calls=%async_computation.3 | async-start | bytes 393216 | tf_op jit(solution)/shard_map/reduce_scatter | solution.py:168
  944.1 30.5 %copy-start.8 = (f32[64,512]{1,0:T(8,128)}, f32[64,512]{1,0:T(8,128)S(1)}, u32[]{:S(2)}) copy-start(f32[64,512]{1,0:T(8,128)S(1)} %maximum_divide_fusion) | copy-start | bytes 393220
  944.2 3.5 collective-permute-start.4
  946.4 4.4 collective-permute-start.5
  950.8 7.9 collective-permute-start.6
  956.1 6.2 collective-permute-start.7
Sparse Core Ops, SparseCore 0:
  919.2 9.8 reduce-scatter.2
  931.3 11.7 reduce-scatter.4
